TPU v7x, 256 devices: a whole 4x4x8 slice. The times are simulated.
256 devices in a mesh: cells: 64 (over z, y, core), tm: 4 (over x).
Axes of the slice: x: 4, y: 4, z: 8, core: 2. Of those that a mesh axis runs over, the one named last changes fastest.
Arguments:
- attitude: float32 [4, 65536], P(None, ('cells', 'tm')), may hold values from -6 to 6
- star_partials: float32 [5, 64, 131072], P(None, None, ('cells', 'tm')), may hold values from -6 to 6
- attitude_partials: float32 [4, 64, 131072], P(None, None, ('cells', 'tm')), may hold values from -6 to 6
- observed: float32 [64, 131072], P(None, ('cells', 'tm')), may hold values from -6 to 6
- phase: float32 [64, 131072], P(None, ('cells', 'tm')), may hold values from 0 to 1
- knot_offset: int32 [64, 131072], P(None, ('cells', 'tm')), may hold values from 0 to 12
- cell_counts: int32 [1024], P(('cells', 'tm')), may hold values from 40 to 64, as said below
- interval_owner: int32 [1024, 64, 1], P(('cells', 'tm')), may hold values from 0 to 255; in each aligned block of 256 rows (0 to 255, 256 to 511, ..., all dimensions but the last counted through in order) at most 2 rows name the same one
- block_slot: int32 [1024, 64], P(('cells', 'tm')), may hold values from 0 to 15
Outputs:
- star_step: float32 [5, 131072], P(None, ('cells', 'tm'))
- attitude_step: float32 [4, 65536], P(None, ('cells', 'tm'))
Inputs may be any that keep to these rules, and one draw needn't show every extreme that they name: `interval_owner`: among the 256 transits of the cells of one device no owner is named more than 2 times, and in every draw some owner is named exactly 2 times by the transits of some device. Transits that are not live are listed too. `cell_counts`: some cell has all 64 transits live in every draw.
All inputs are finite; a program needn't handle non-finite values.
Results may differ from a plain program's by a relative error of at most 0.0003.
Values sent between devices are 32-bit elements; how exact they have to be, the bound alone decides.
A program may use at most 128 MiB of HBM per device.

v0:
```python
import jax
import jax.numpy as jnp
from jax import lax
from jax.sharding import PartitionSpec as P

CS = 128
KB = 16
ITERS = 6
smoothing = 16.0
damping = 2.0
relaxation = 0.5
star_prior = 1.0
highest = lax.Precision.HIGHEST


def padded_2(shard, sides, width):
    for axis, dim in sides:
        size, length = (lax.axis_size(axis), shard.shape[dim])
        up = [(i, (i + 1) % size) for i in range(size - 1)]
        down = [(j, i) for i, j in up]
        last = lax.slice_in_dim(shard, length - width, length, axis=dim)
        leading = lax.slice_in_dim(shard, 0, width, axis=dim)
        before = lax.ppermute(last, axis, up)
        after = lax.ppermute(leading, axis, down)
        shard = jnp.concatenate([before, shard, after], axis=dim)
    return shard


def spline_basis(phase):
    square = phase * phase
    cube = square * phase
    rest = 1.0 - phase
    return (
        rest * rest * rest / 6.0,
        (3.0 * cube - 6.0 * square + 4.0) / 6.0,
        (-3.0 * cube + 3.0 * square + 3.0 * phase + 1.0) / 6.0,
        cube / 6.0,
    )


def design_rows(phase, knot_offset, partials, live):
    knots = lax.broadcasted_iota(jnp.int32, (KB, 1), 0)
    basis = spline_basis(phase)
    spread = jnp.zeros(phase.shape[:-1] + (KB, phase.shape[-1]), jnp.float32)
    for order in range(4):
        hit = knots == knot_offset[..., None, :] + order
        spread = spread + jnp.where(hit, basis[order][..., None, :], 0.0)
    spread = spread * live[..., None, None]
    return jnp.moveaxis(partials, 0, -2)[..., :, None, :] * spread[..., None, :, :]


def cholesky_factor(matrix, size):
    lower = [[None for column in range(size)] for row in range(size)]
    for column in range(size):
        total = matrix[column][column]
        for inner in range(column):
            total = total - lower[column][inner] * lower[column][inner]
        pivot = jnp.sqrt(total)
        lower[column][column] = pivot
        for row in range(column + 1, size):
            accum = matrix[row][column]
            for inner in range(column):
                accum = accum - lower[row][inner] * lower[column][inner]
            lower[row][column] = accum / pivot
    return lower


def cholesky_solve(lower, rhs, size):
    forward = []
    for row in range(size):
        accum = rhs[row]
        for inner in range(row):
            accum = accum - lower[row][inner] * forward[inner]
        forward.append(accum / lower[row][row])
    answer = [None for row in range(size)]
    for row in reversed(range(size)):
        accum = forward[row]
        for inner in range(row + 1, size):
            accum = accum - lower[inner][row] * answer[inner]
        answer[row] = accum / lower[row][row]
    return answer


def star_update(partials, first, live):
    normal = [
        [
            jnp.sum(live * partials[row] * partials[column], axis=0)
            + (star_prior if row == column else 0.0)
            for column in range(5)
        ]
        for row in range(5)
    ]
    rhs = [jnp.sum(partials[row] * first, axis=0) for row in range(5)]
    lower = cholesky_factor(normal, 5)
    step = cholesky_solve(lower, rhs, 5)
    fitted = partials[0] * step[0]
    for row in range(1, 5):
        fitted = fitted + partials[row] * step[row]
    return (jnp.stack(step), first - live * fitted)


def dense_to_band(dense):
    pieces = []
    for shift in range(4):
        diagonal = jnp.diagonal(dense, offset=shift, axis1=2, axis2=4)
        filler = jnp.zeros(diagonal.shape[:-1] + (shift,), jnp.float32)
        pieces.append(jnp.concatenate([diagonal, filler], axis=-1))
    return jnp.stack(pieces, axis=-2)


def band_apply(band, vector):
    result = jnp.einsum("bmna,nba->mba", band[:, :, :, 0, :], vector, precision=highest)
    for shift in range(1, 4):
        filler = jnp.zeros(vector.shape[:-1] + (shift,), jnp.float32)
        ahead = jnp.concatenate([vector[..., shift:], filler], axis=-1)
        result = result + jnp.einsum(
            "bmna,nba->mba", band[:, :, :, shift, :], ahead, precision=highest
        )
        lagged = jnp.einsum("bnma,nba->mba", band[:, :, :, shift, :], vector, precision=highest)
        result = result + jnp.concatenate([filler, lagged[..., : KB - shift]], axis=-1)
    return result


def diagonal_factor(band):
    shifted = 2.0 * smoothing + damping
    entries = [
        [band[:, row, column, 0, :] + (shifted if row == column else 0.0) for column in range(4)]
        for row in range(4)
    ]
    return cholesky_factor(entries, 4)


def sweep(band, lower, gradient, solution, padded):
    count = band.shape[0]
    applied = band_apply(band, solution.reshape(4, count, KB))
    regular = smoothing * (2.0 * solution - padded[:, :-2] - padded[:, 2:]) + damping * solution
    misfit = gradient - applied - regular.reshape(4, count, KB)
    correction = cholesky_solve(lower, [misfit[row] for row in range(4)], 4)
    return solution + relaxation * jnp.stack(correction).reshape(4, count * KB)


def cell_work(items):
    cell_phase, cell_offset, cell_axis, cell_star, cell_observed, cell_live, cell_values = items
    rows = design_rows(cell_phase, cell_offset, cell_axis, cell_live)
    predicted = jnp.einsum("tmas,tma->ts", rows, cell_values, precision=highest)
    first = cell_live[:, None] * cell_observed - predicted
    step, second = star_update(cell_star, first, cell_live[:, None])
    gradient = jnp.einsum("tmas,ts->tma", rows, second, precision=highest)
    flat = rows.reshape(rows.shape[0], 4 * KB, rows.shape[-1])
    normal = jnp.einsum("tis,tks->tik", flat, flat, precision=highest).reshape(
        rows.shape[0], 16 * KB * KB
    )
    return (step, normal, gradient.reshape(rows.shape[0], 4 * KB))


def per_device(
    attitude,
    star_partials,
    attitude_partials,
    observed,
    phase,
    knot_offset,
    cell_counts,
    interval_owner,
    block_slot,
):
    cell_groups = lax.axis_size("cells")
    time_groups = lax.axis_size("tm")
    devices = cell_groups * time_groups
    cells_here = cell_counts.shape[0]
    transits = observed.shape[0]
    blocks_here = attitude.shape[1] // KB
    total = cells_here * transits
    capacity = max(2, 3 * total // (2 * devices))
    owners = interval_owner.reshape(total)
    slots = block_slot.reshape(total)
    order = lax.broadcasted_iota(jnp.int32, (total, total), 0)
    other = lax.broadcasted_iota(jnp.int32, (total, total), 1)
    same = (owners[:, None] == owners[None, :]) & (other < order)
    rank = jnp.sum(same.astype(jnp.int32), axis=1)
    position = owners * capacity + rank
    requests = jnp.zeros((devices * capacity,), jnp.int32).at[position].set(slots)
    requested = lax.all_to_all(
        lax.all_to_all(
            requests.reshape(cell_groups, time_groups, capacity),
            "cells",
            split_axis=0,
            concat_axis=0,
            tiled=True,
        ),
        "tm",
        split_axis=1,
        concat_axis=1,
        tiled=True,
    )
    whole = lax.all_gather(attitude, ("cells", "tm"), axis=1, tiled=True)
    global_ids = owners * blocks_here + slots
    values = whole.reshape(4, -1, KB)[:, global_ids, :].transpose(1, 0, 2)
    transit = lax.broadcasted_iota(jnp.int32, (cells_here, transits), 1)
    live = jnp.where(transit < cell_counts[:, None], 1.0, 0.0).astype(jnp.float32)
    items = (
        phase.reshape(transits, cells_here, CS).transpose(1, 0, 2),
        knot_offset.reshape(transits, cells_here, CS).transpose(1, 0, 2),
        attitude_partials.reshape(4, transits, cells_here, CS).transpose(2, 0, 1, 3),
        star_partials.reshape(5, transits, cells_here, CS).transpose(2, 0, 1, 3),
        observed.reshape(transits, cells_here, CS).transpose(1, 0, 2),
        live,
        values.reshape(cells_here, transits, 4, KB),
    )
    steps, normals, gradients = lax.map(cell_work, items)
    payload = normals.reshape(total, normals.shape[-1])
    gradient_rows = gradients.reshape(total, 4 * KB)
    outgoing = (
        jnp.zeros((devices * capacity, payload.shape[1]), jnp.float32).at[position].set(payload)
    )
    outgoing_grad = (
        jnp.zeros((devices * capacity, 4 * KB), jnp.float32).at[position].set(gradient_rows)
    )
    arrived, arrived_grad = (
        lax.all_to_all(
            lax.all_to_all(
                outgoing.reshape(cell_groups, time_groups, capacity, payload.shape[1]),
                "cells",
                split_axis=0,
                concat_axis=0,
                tiled=True,
            ),
            "tm",
            split_axis=1,
            concat_axis=1,
            tiled=True,
        ),
        lax.all_to_all(
            lax.all_to_all(
                outgoing_grad.reshape(cell_groups, time_groups, capacity, 4 * KB),
                "cells",
                split_axis=0,
                concat_axis=0,
                tiled=True,
            ),
            "tm",
            split_axis=1,
            concat_axis=1,
            tiled=True,
        ),
    )
    member_rows = lax.broadcasted_iota(jnp.int32, (blocks_here, devices * capacity), 0)
    member = (member_rows == requested.reshape(1, devices * capacity)).astype(jnp.float32)
    block_normal = jnp.dot(
        member,
        arrived.reshape(devices * capacity, payload.shape[1]),
        precision=highest,
        preferred_element_type=jnp.float32,
    )
    block_grad = jnp.dot(
        member,
        arrived_grad.reshape(devices * capacity, 4 * KB),
        precision=highest,
        preferred_element_type=jnp.float32,
    )
    band = dense_to_band(block_normal.reshape(blocks_here, 4, KB, 4, KB))
    gradient = block_grad.reshape(blocks_here, 4, KB).transpose(1, 0, 2)
    lower = diagonal_factor(band)
    solution = jnp.zeros((4, blocks_here * KB), jnp.float32)
    for index in range(ITERS):
        padded = padded_2(solution, ((("cells", "tm"), 1),), 1)
        solution = sweep(band, lower, gradient, solution, padded)
    star_step = steps.transpose(1, 0, 2).reshape(5, cells_here * CS)
    return (star_step, solution)


def solution(mesh):
    placed = (
        P(None, ("cells", "tm")),
        P(None, None, ("cells", "tm")),
        P(None, None, ("cells", "tm")),
        P(None, ("cells", "tm")),
        P(None, ("cells", "tm")),
        P(None, ("cells", "tm")),
        P(("cells", "tm")),
        P(("cells", "tm"), None, None),
        P(("cells", "tm"), None),
    )
    return jax.shard_map(
        per_device,
        mesh=mesh,
        in_specs=placed,
        out_specs=(P(None, ("cells", "tm")), P(None, ("cells", "tm"))),
        check_vma=False,
    )
```

profile of v0, /device:TPU:127, one launch (start us, length us, event | category | flops | bytes accessed | tf_op | source)
XLA Modules:
  0.0 741.4 jit_solution(1246843753524124529)
XLA Ops:
  14.2 10.9 %all-to-all-start = ((s32[64,4,2]{1,2,0:T(2,128)}), s32[64,4,2]{1,2,0:T(2,128)S(1)}, u32[]{:S(2)}, u32[]{:S(2)}) async-start(s32[64,4,2]{1,2,0:T(2,128)} %copy.75), calls=%async_computation | async-start | bytes 131072 | tf_op jit(solution)/shard_map/all_to_all | solution.py:184
  35.7 4.2 all-to-all-start.1
  39.9 75.8 %all-gather.2.cloned.1.call-done = f32[4,65536]{1,0:T(4,128)} async-done(((f32[4,256]{1,0:T(4,128)}), f32[4,65536]{1,0:T(4,128)}) %all-gather.2.cloned.1.call-update) | async-done | bytes 1048592 | tf_op jit(solution)/shard_map/all_gather | solution.py:196
  115.7 7.3 reshape.1760
  123.1 11.8 %copy.67 = f32[4,4096,16]{2,0,1:T(4,128)} copy(f32[4,4096,16]{2,1,0:T(8,128)} %reshape.1760) | data formatting | bytes 2097152 | tf_op jit(solution)/shard_map/reshape | solution.py:198
  134.9 4.4 gather_fusion
  139.5 125.9 %while.14 = (s32[]{:T(128)}, f32[4,5,128]{2,1,0:T(8,128)}, f32[4,64,4096]{2,1,0:T(8,128)}, f32[4,64,64]{2,1,0:T(8,128)}, f32[4,5,64,128]{3,0,2,1:T(4,128)}, /*in...) while((s32[]{:T(128)}, f32[4,5,128]{2,1,0:T(8,128)}, ...), condition=%wide.region_21.22_spmd, body=%wide.region_0.21_spmd.sunk | while | flops 419069696 | bytes 14432589 | solution.py:210
  147.6 14.7 %fusion.269 = f32[64,1,4,16]{3,1,2,0:T(1,128)S(1)} fusion(f32[64,128,1,1]{1,2,3,0:T(1,128)S(1)} %bitcast.973, f32[64,16,128]{2,1,0:T(8,128)S(1)} %add_multiply_fusion.2, f32[64,4,128]{2,1,0:T(4,128)S(1)} %bitcast.953), kind=kOutput, calls=%fused_computation.8.clone.1 | convolution fusion | flops 6815744 | bytes 704512 | tf_op jit(solution)/shard_map/while/body/eval_jaxpr/tmas,ts->tma/dot_general | solution.py:148
  163.3 3.4 fusion.268
  178.8 14.7 %fusion.269 = f32[64,1,4,16]{3,1,2,0:T(1,128)S(1)} fusion(f32[64,128,1,1]{1,2,3,0:T(1,128)S(1)} %bitcast.973, f32[64,16,128]{2,1,0:T(8,128)S(1)} %add_multiply_fusion.2, f32[64,4,128]{2,1,0:T(4,128)S(1)} %bitcast.953), kind=kOutput, calls=%fused_computation.8.clone.1 | convolution fusion | flops 6815744 | bytes 704512 | tf_op jit(solution)/shard_map/while/body/eval_jaxpr/tmas,ts->tma/dot_general | solution.py:148
  210.2 14.7 %fusion.269 = f32[64,1,4,16]{3,1,2,0:T(1,128)S(1)} fusion(f32[64,128,1,1]{1,2,3,0:T(1,128)S(1)} %bitcast.973, f32[64,16,128]{2,1,0:T(8,128)S(1)} %add_multiply_fusion.2, f32[64,4,128]{2,1,0:T(4,128)S(1)} %bitcast.953), kind=kOutput, calls=%fused_computation.8.clone.1 | convolution fusion | flops 6815744 | bytes 704512 | tf_op jit(solution)/shard_map/while/body/eval_jaxpr/tmas,ts->tma/dot_general | solution.py:148
  241.5 14.7 %fusion.269 = f32[64,1,4,16]{3,1,2,0:T(1,128)S(1)} fusion(f32[64,128,1,1]{1,2,3,0:T(1,128)S(1)} %bitcast.973, f32[64,16,128]{2,1,0:T(8,128)S(1)} %add_multiply_fusion.2, f32[64,4,128]{2,1,0:T(4,128)S(1)} %bitcast.953), kind=kOutput, calls=%fused_computation.8.clone.1 | convolution fusion | flops 6815744 | bytes 704512 | tf_op jit(solution)/shard_map/while/body/eval_jaxpr/tmas,ts->tma/dot_general | solution.py:148
  267.8 8.8 %all-to-all-start.2 = ((f32[64,1,512]{2,1,0:T(1,128)}), f32[64,1,512]{2,1,0:T(1,128)S(1)}, u32[]{:S(2)}, u32[]{:S(2)}) async-start(f32[64,1,512]{2,1,0:T(1,128)} %reshape.1951), calls=%async_computation.2 | async-start | bytes 262144 | tf_op jit(solution)/shard_map/all_to_all | solution.py:234
  276.7 8.2 %scatter_custom_fusion.2 = f32[512,4096]{1,0:T(8,128)} fusion(s32[256]{0:T(256)} %bitcast.1001, f32[256,4096]{1,0:T(8,128)} %bitcast.1002, f32[]{:T(128)} %constant.54.clone.1), kind=kCustom, calls=%fused_computation.167 | custom fusion | bytes 8389120 | tf_op jit(solution)/shard_map/scatter | solution.py:214
  284.9 10.6 %reshape.1770 = f32[64,4,2,4096]{3,2,1,0:T(2,128)} reshape(f32[512,4096]{1,0:T(8,128)} %scatter_custom_fusion.2) | data formatting | bytes 16777216 | tf_op jit(solution)/shard_map/reshape | solution.py:222
  295.5 10.5 %all-to-all-start.4 = ((f32[64,4,2,4096]{3,2,1,0:T(2,128)}), f32[64,4,2,4096]{3,2,1,0:T(2,128)}, u32[]{:S(2)}, u32[]{:S(2)}) async-start(f32[64,4,2,4096]{3,2,1,0:T(2,128)} %reshape.1770), calls=%async_computation.4 | async-start | bytes 16777216 | tf_op jit(solution)/shard_map/all_to_all | solution.py:221
  308.6 178.9 %all-to-all-done.4 = f32[64,4,2,4096]{3,2,1,0:T(2,128)} async-done(((f32[64,4,2,4096]{3,2,1,0:T(2,128)}), f32[64,4,2,4096]{3,2,1,0:T(2,128)}, u32[]{:S(2)}, u32[]{:S(2)}) %all-to-all-start.4) | async-done | bytes 8388640 | tf_op jit(solution)/shard_map/all_to_all | solution.py:221
  487.6 4.2 all-to-all-start.3
  491.8 7.4 copy.83
  499.2 5.7 all-to-all-start.5
  510.2 85.5 %collective-permute-done = f32[4,1]{1,0:T(4,128)S(1)} collective-permute-done((f32[4,1]{1,0:T(4,128)S(1)}, f32[4,1]{1,0:T(4,128)S(1)}, u32[]{:S(2)}, u32[]{:S(2)}) %collective-permute-start) | collective-permute-done | bytes 48 | tf_op jit(solution)/shard_map/ppermute | solution.py:23
  599.8 7.6 %copy.84 = f32[64,4,2,4096]{3,2,1,0:T(2,128)} copy(f32[64,4,2,4096]{3,2,0,1:T(2,128)} %all-to-all-done.5) | data formatting | bytes 16777216 | tf_op jit(solution)/shard_map/all_to_all | solution.py:220
  607.4 10.9 %reshape.1771 = f32[512,4096]{1,0:T(8,128)} reshape(f32[64,4,2,4096]{3,2,1,0:T(2,128)} %copy.84) | data formatting | bytes 16777216 | tf_op jit(solution)/shard_map/reshape | solution.py:251
  618.3 9.0 %copy.85 = f32[4096,512]{1,0:T(8,128)} copy(f32[4096,512]{0,1:T(8,128)} %bitcast.915) | data formatting | bytes 16777216 | tf_op jit(solution)/shard_map/dot_general | solution.py:249
  627.3 17.0 %convolution_bitcast_fusion = f32[16,4,4,16,16]{4,0,2,3,1:T(8,128)S(1)} fusion(f32[4,16,4,16,512]{4,3,2,1,0:T(8,128)} %bitcast.914, s32[512]{0:T(512)S(1)} %eq.99), kind=kOutput, calls=%fused_computation.169 | convolution fusion | flops 402661376 | bytes 8652800 | tf_op jit(solution)/shard_map/dot_general | solution.py:249
  658.6 5.3 collective-permute-start.2
  665.9 8.4 %collective-permute-done.3 = f32[4,1]{1,0:T(4,128)S(1)} collective-permute-done((f32[4,1]{1,0:T(4,128)S(1)}, f32[4,1]{1,0:T(4,128)S(1)}, u32[]{:S(2)}, u32[]{:S(2)}) %collective-permute-start.3) | collective-permute-done | bytes 48 | tf_op jit(solution)/shard_map/ppermute | solution.py:24
  682.0 7.0 collective-permute-done.5
  693.3 3.6 collective-permute-start.7
  696.9 6.7 collective-permute-done.7
  711.3 7.0 collective-permute-done.9
  726.0 7.0 collective-permute-done.11
  (509 shorter events, 138.6 us)
Async XLA Ops:
  7.2 108.6 %all-gather.2.cloned.1.call-start = ((), (), s32[]{:S(2)}) async-start(), calls=%async_computation.6 | async-start | bytes 1052672 | tf_op jit(solution)/shard_map/all_gather | solution.py:196
  10.9 0.6 copy-start.16
  14.2 20.7 %all-to-all-start = ((s32[64,4,2]{1,2,0:T(2,128)}), s32[64,4,2]{1,2,0:T(2,128)S(1)}, u32[]{:S(2)}, u32[]{:S(2)}) async-start(s32[64,4,2]{1,2,0:T(2,128)} %copy.75), calls=%async_computation | async-start | bytes 131072 | tf_op jit(solution)/shard_map/all_to_all | solution.py:184
  35.7 232.2 %all-to-all-start.1 = ((s32[4,1,128]{2,1,0:T(1,128)}), s32[4,1,128]{2,1,0:T(1,128)}, u32[]{:S(2)}, u32[]{:S(2)}) async-start(s32[4,1,128]{2,1,0:T(1,128)} %reshape.1949), calls=%async_computation.1 | async-start | bytes 4096 | tf_op jit(solution)/shard_map/all_to_all | solution.py:183
  146.8 0.6 copy-start.1
  146.9 0.6 copy-start.2
  146.9 0.6 copy-start.7
  146.9 0.6 copy-start.8
  178.1 0.6 copy-start.1
  178.1 0.6 copy-start.2
  178.2 0.6 copy-start.7
  178.2 0.6 copy-start.8
  209.5 0.6 copy-start.1
  209.5 0.6 copy-start.7
  240.7 0.6 copy-start.1
  240.8 0.6 copy-start.7
  267.8 27.6 %all-to-all-start.2 = ((f32[64,1,512]{2,1,0:T(1,128)}), f32[64,1,512]{2,1,0:T(1,128)S(1)}, u32[]{:S(2)}, u32[]{:S(2)}) async-start(f32[64,1,512]{2,1,0:T(1,128)} %reshape.1951), calls=%async_computation.2 | async-start | bytes 262144 | tf_op jit(solution)/shard_map/all_to_all | solution.py:234
  295.5 192.1 %all-to-all-start.4 = ((f32[64,4,2,4096]{3,2,1,0:T(2,128)}), f32[64,4,2,4096]{3,2,1,0:T(2,128)}, u32[]{:S(2)}, u32[]{:S(2)}) async-start(f32[64,4,2,4096]{3,2,1,0:T(2,128)} %reshape.1770), calls=%async_computation.4 | async-start | bytes 16777216 | tf_op jit(solution)/shard_map/all_to_all | solution.py:221
  487.6 11.6 %all-to-all-start.3 = ((f32[4,1,8192]{2,1,0:T(1,128)}), f32[4,1,8192]{2,1,0:T(1,128)S(1)}, u32[]{:S(2)}, u32[]{:S(2)}) async-start(f32[4,1,8192]{2,1,0:T(1,128)} %reshape.1953), calls=%async_computation.3 | async-start | bytes 262144 | tf_op jit(solution)/shard_map/all_to_all | solution.py:233
  499.2 100.6 %all-to-all-start.5 = ((f32[64,4,2,4096]{3,2,0,1:T(2,128)}), f32[64,4,2,4096]{3,2,0,1:T(2,128)}, u32[]{:S(2)}, u32[]{:S(2)}) async-start(f32[64,4,2,4096]{3,2,0,1:T(2,128)} %copy.83), calls=%async_computation.5 | async-start | bytes 16777216 | tf_op jit(solution)/shard_map/all_to_all | solution.py:220
  504.9 90.9 %collective-permute-start = (f32[4,1]{1,0:T(4,128)S(1)}, f32[4,1]{1,0:T(4,128)S(1)}, u32[]{:S(2)}, u32[]{:S(2)}) collective-permute-start(f32[4,1]{1,0:T(4,128)S(1)} %broadcast.741), channel_id=1, source_target_pairs={{0,1},{1,2},{2,3},{3,4},{4,5},{5,6},{6,7},{7,8},{8,9},{9,10},{10,1... | collective-permute-start | bytes 56 | tf_op jit(solution)/shard_map/ppermute | solution.py:23
  508.2 87.5 %collective-permute-start.1 = (f32[4,1]{1,0:T(4,128)S(1)}, f32[4,1]{1,0:T(4,128)S(1)}, u32[]{:S(2)}, u32[]{:S(2)}) collective-permute-start(f32[4,1]{1,0:T(4,128)S(1)} %broadcast.741), channel_id=1, source_target_pairs={{1,0},{2,1},{3,2},{4,3},{5,4},{6,5},{7,6},{8,7},{9,8},{10,9},{11,1... | collective-permute-start | bytes 56 | tf_op jit(solution)/shard_map/ppermute | solution.py:24
  658.6 7.3 collective-permute-start.2
  664.0 10.3 %collective-permute-start.3 = (f32[4,1]{1,0:T(4,128)S(1)}, f32[4,1]{1,0:T(4,128)S(1)}, u32[]{:S(2)}, u32[]{:S(2)}) collective-permute-start(f32[4,1]{1,0:T(4,128)S(1)} %get-tuple-element.277), channel_id=1, source_target_pairs={{1,0},{2,1},{3,2},{4,3},{5,4},{6,5},{7,6},{8,7},{9,8},{10,9},{11,1... | collective-permute-start | bytes 56 | tf_op jit(solution)/shard_map/ppermute | solution.py:24
  676.7 5.3 collective-permute-start.4
  678.6 10.3 %collective-permute-start.5 = (f32[4,1]{1,0:T(4,128)S(1)}, f32[4,1]{1,0:T(4,128)S(1)}, u32[]{:S(2)}, u32[]{:S(2)}) collective-permute-start(f32[4,1]{1,0:T(4,128)S(1)} %get-tuple-element.275), channel_id=1, source_target_pairs={{1,0},{2,1},{3,2},{4,3},{5,4},{6,5},{7,6},{8,7},{9,8},{10,9},{11,1... | collective-permute-start | bytes 56 | tf_op jit(solution)/shard_map/ppermute | solution.py:24
  691.3 5.5 collective-permute-start.6
  693.3 10.3 %collective-permute-start.7 = (f32[4,1]{1,0:T(4,128)S(1)}, f32[4,1]{1,0:T(4,128)S(1)}, u32[]{:S(2)}, u32[]{:S(2)}) collective-permute-start(f32[4,1]{1,0:T(4,128)S(1)} %get-tuple-element.273), channel_id=1, source_target_pairs={{1,0},{2,1},{3,2},{4,3},{5,4},{6,5},{7,6},{8,7},{9,8},{10,9},{11,1... | collective-permute-start | bytes 56 | tf_op jit(solution)/shard_map/ppermute | solution.py:24
  706.0 5.3 collective-permute-start.8
  708.0 10.3 %collective-permute-start.9 = (f32[4,1]{1,0:T(4,128)S(1)}, f32[4,1]{1,0:T(4,128)S(1)}, u32[]{:S(2)}, u32[]{:S(2)}) collective-permute-start(f32[4,1]{1,0:T(4,128)S(1)} %get-tuple-element.271), channel_id=1, source_target_pairs={{1,0},{2,1},{3,2},{4,3},{5,4},{6,5},{7,6},{8,7},{9,8},{10,9},{11,1... | collective-permute-start | bytes 56 | tf_op jit(solution)/shard_map/ppermute | solution.py:24
  720.7 5.3 collective-permute-start.10
  722.7 10.3 %collective-permute-start.11 = (f32[4,1]{1,0:T(4,128)S(1)}, f32[4,1]{1,0:T(4,128)S(1)}, u32[]{:S(2)}, u32[]{:S(2)}) collective-permute-start(f32[4,1]{1,0:T(4,128)S(1)} %get-tuple-element.269), channel_id=1, source_target_pairs={{1,0},{2,1},{3,2},{4,3},{5,4},{6,5},{7,6},{8,7},{9,8},{10,9},{11,1... | collective-permute-start | bytes 56 | tf_op jit(solution)/shard_map/ppermute | solution.py:24
  (52 other events, 29.4 us)
Sparse Core Ops, SparseCore 0:
  11.7 103.9 all-gather.1
where the time goes:
time: 751 us; the launch traced here: 741 us
  waiting for transfers between devices  377 us (50%)
  local copies, waits for them, and re-layouts  148 us (20%)
  matrix products  97.9 us (13%)
  starting transfers between devices  78.2 us (10%)
  other arithmetic  23.7 us (3%)
  between operations  15.1 us (2%)
    all_to_all x1, waiting for transfers between devices, per_device(): lax.all_to_all(outgoing.reshape(cell_groups, time_groups, capacity, paylo...  179 us
    ppermute x6, waiting for transfers between devices, padded_2(): before = lax.ppermute(last, axis, up)  85.5 us
    all_gather x1, waiting for transfers between devices, per_device(): whole = lax.all_gather(attitude, ('cells', 'tm'), axis=1, tiled=True)  75.8 us
    dot_general x4, matrix products, cell_work(): gradient = jnp.einsum('tmas,ts->tma', rows, second, precision=highest)  58.7 us
    ppermute x6, waiting for transfers between devices, padded_2(): after = lax.ppermute(leading, axis, down)  36.1 us
    reshape x2, local copies, waits for them, and re-layouts, per_device(): values = whole.reshape(4, -1, KB)[:, global_ids, :].transpose(1, 0, 2)  19.2 us
    ppermute x6, starting transfers between devices, padded_2(): after = lax.ppermute(leading, axis, down)  17.4 us
    dot_general x1, matrix products, per_device(): jnp.dot(member, arrived.reshape(devices * capacity, payload.shape[1]), pr...  17 us
  transfers between devices with their start and end apart: 19, of which 8 were waited for; matrix products, arithmetic and copies ran while one was open for 27% of the time, Pallas kernels for 0%

commit v1 on v0

--- a/solution.py
+++ b/solution.py
@@ -193,7 +193,10 @@
         concat_axis=1,
         tiled=True,
     )
-    whole = lax.all_gather(attitude, ("cells", "tm"), axis=1, tiled=True)
+    n_dev = lax.axis_size(("cells", "tm"))
+    parts = jnp.stack([attitude for _ in range(n_dev)])
+    parts = lax.all_to_all(parts, ("cells", "tm"), split_axis=0, concat_axis=0)
+    whole = jnp.concatenate(parts, axis=1)
     global_ids = owners * blocks_here + slots
     values = whole.reshape(4, -1, KB)[:, global_ids, :].transpose(1, 0, 2)
     transit = lax.broadcasted_iota(jnp.int32, (cells_here, transits), 1)

time: 751 us -> 692 us (0.921)
  waiting for transfers between devices: 377 us -> 320 us
  blocking collectives: 0 us -> 16.3 us
  between operations: 15.1 us -> 1.74 us
    all_gather x1 -> x0, waiting for transfers between devices: 75.8 us -> none  [per_device(): whole = lax.all_gather(attitude, ('cells', 'tm'), axis=1, tiled=True)]
    all_to_all x1, waiting for transfers between devices: 0.01 us -> 19 us  [per_device(): parts = lax.all_to_all(parts, ('cells', 'tm'), split_axis=0, concat_axis=0)]
    reshape x2 -> x1, local copies, waits for them, and re-layouts: 19.2 us -> 0.2 us  [per_device(): whole = jnp.concatenate(parts, axis=1)]
    another operation x1 -> x4, local copies, waits for them, and re-layouts: 0.01 us -> 18.3 us  [the longest x2 16.5 us: per_device(): values = whole.reshape(4, -1, KB)[:, global_ids, :].transpose(1, 0, 2)]
    all_to_all x0 -> x1, blocking collectives: none -> 16.3 us  [per_device(): lax.all_to_all(requests.reshape(cell_groups, time_groups, capacity), 'cel...]
  transfers between devices with their start and end apart: 19 -> 18, of which waited for: 8 -> 8; matrix products, arithmetic and copies ran while one was open for 27% -> 27% of each run, Pallas kernels for 0% -> 0%
where the time goes in v1:
time: 692 us; the launch traced here: 683 us
  waiting for transfers between devices  320 us (46%)
  local copies, waits for them, and re-layouts  143 us (21%)
  matrix products  97.9 us (14%)
  starting transfers between devices  80.1 us (12%)
  other arithmetic  23 us (3%)
  blocking collectives  16.3 us (2%)
    all_to_all x1, waiting for transfers between devices, per_device(): lax.all_to_all(outgoing.reshape(cell_groups, time_groups, capacity, paylo...  179 us
    ppermute x6, waiting for transfers between devices, padded_2(): before = lax.ppermute(last, axis, up)  85.5 us
    dot_general x4, matrix products, cell_work(): gradient = jnp.einsum('tmas,ts->tma', rows, second, precision=highest)  58.7 us
    ppermute x6, waiting for transfers between devices, padded_2(): after = lax.ppermute(leading, axis, down)  36.1 us
    all_to_all x1, waiting for transfers between devices, per_device(): parts = lax.all_to_all(parts, ('cells', 'tm'), split_axis=0, concat_axis=0)  19 us
    ppermute x6, starting transfers between devices, padded_2(): after = lax.ppermute(leading, axis, down)  17.4 us
    dot_general x1, matrix products, per_device(): jnp.dot(member, arrived.reshape(devices * capacity, payload.shape[1]), pr...  17 us
    another operation x2, local copies, waits for them, and re-layouts, per_device(): values = whole.reshape(4, -1, KB)[:, global_ids, :].transpose(1, 0, 2)  16.5 us
  transfers between devices with their start and end apart: 18, of which 8 were waited for; matrix products, arithmetic and copies ran while one was open for 27% of the time, Pallas kernels for 0%

profile of v1, /device:TPU:127, one launch (start us, length us, event | category | flops | bytes accessed | tf_op | source)
XLA Modules:
  0.0 683.1 jit_solution(2052122918424182578)
XLA Ops:
  6.4 16.3 %all_to_all.35 = s32[64,4,2]{1,2,0:T(2,128)S(1)} all-to-all(s32[64,4,2]{1,2,0:T(2,128)S(1)} %copy.77), channel_id=1, replica_groups=mesh['cells'=64,'tm'=4] {'cells'}, dimensions={0} | all-to-all | bytes 4096 | tf_op jit(solution)/shard_map/all_to_all | solution.py:184
  24.5 11.3 %all-to-all-start = ((f32[256,4,256]{2,1,0:T(4,128)}), f32[256,4,256]{2,1,0:T(4,128)S(1)}, u32[]{:S(2)}, u32[]{:S(2)}) async-start(f32[256,4,256]{2,1,0:T(4,128)} %stack.76), calls=%async_computation | async-start | bytes 2097152 | tf_op jit(solution)/shard_map/all_to_all | solution.py:198
  42.0 19.0 %all-to-all-done = f32[256,4,256]{2,1,0:T(4,128)S(1)} async-done(((f32[256,4,256]{2,1,0:T(4,128)}), f32[256,4,256]{2,1,0:T(4,128)S(1)}, u32[]{:S(2)}, u32[]{:S(2)}) %all-to-all-start) | async-done | bytes 1048608 | tf_op jit(solution)/shard_map/all_to_all | solution.py:198
  61.1 6.1 all-to-all-start.2
  67.3 4.7 reshape_reshape.3
  72.0 11.8 %copy.69 = f32[4,4096,16]{2,0,1:T(4,128)} copy(f32[4,4096,16]{2,1,0:T(8,128)} %reshape_reshape.3) | data formatting | bytes 2097152 | tf_op jit(solution)/shard_map/reshape;reshape | solution.py:201
  83.8 4.4 gather_fusion
  88.4 125.9 %while.14 = (s32[]{:T(128)}, f32[4,5,128]{2,1,0:T(8,128)}, f32[4,64,4096]{2,1,0:T(8,128)}, f32[4,64,64]{2,1,0:T(8,128)}, f32[4,5,64,128]{3,0,2,1:T(4,128)}, /*in...) while((s32[]{:T(128)}, f32[4,5,128]{2,1,0:T(8,128)}, ...), condition=%wide.region_21.22_spmd, body=%wide.region_0.21_spmd.sunk | while | flops 419069696 | bytes 14432589 | solution.py:213
  96.5 14.7 %fusion.269 = f32[64,1,4,16]{3,1,2,0:T(1,128)S(1)} fusion(f32[64,128,1,1]{1,2,3,0:T(1,128)S(1)} %bitcast.975, f32[64,16,128]{2,1,0:T(8,128)S(1)} %add_multiply_fusion.2, f32[64,4,128]{2,1,0:T(4,128)S(1)} %bitcast.954), kind=kOutput, calls=%fused_computation.8.clone.1 | convolution fusion | flops 6815744 | bytes 704512 | tf_op jit(solution)/shard_map/while/body/eval_jaxpr/tmas,ts->tma/dot_general | solution.py:148
  127.8 14.7 %fusion.269 = f32[64,1,4,16]{3,1,2,0:T(1,128)S(1)} fusion(f32[64,128,1,1]{1,2,3,0:T(1,128)S(1)} %bitcast.975, f32[64,16,128]{2,1,0:T(8,128)S(1)} %add_multiply_fusion.2, f32[64,4,128]{2,1,0:T(4,128)S(1)} %bitcast.954), kind=kOutput, calls=%fused_computation.8.clone.1 | convolution fusion | flops 6815744 | bytes 704512 | tf_op jit(solution)/shard_map/while/body/eval_jaxpr/tmas,ts->tma/dot_general | solution.py:148
  159.1 14.7 %fusion.269 = f32[64,1,4,16]{3,1,2,0:T(1,128)S(1)} fusion(f32[64,128,1,1]{1,2,3,0:T(1,128)S(1)} %bitcast.975, f32[64,16,128]{2,1,0:T(8,128)S(1)} %add_multiply_fusion.2, f32[64,4,128]{2,1,0:T(4,128)S(1)} %bitcast.954), kind=kOutput, calls=%fused_computation.8.clone.1 | convolution fusion | flops 6815744 | bytes 704512 | tf_op jit(solution)/shard_map/while/body/eval_jaxpr/tmas,ts->tma/dot_general | solution.py:148
  190.4 14.7 %fusion.269 = f32[64,1,4,16]{3,1,2,0:T(1,128)S(1)} fusion(f32[64,128,1,1]{1,2,3,0:T(1,128)S(1)} %bitcast.975, f32[64,16,128]{2,1,0:T(8,128)S(1)} %add_multiply_fusion.2, f32[64,4,128]{2,1,0:T(4,128)S(1)} %bitcast.954), kind=kOutput, calls=%fused_computation.8.clone.1 | convolution fusion | flops 6815744 | bytes 704512 | tf_op jit(solution)/shard_map/while/body/eval_jaxpr/tmas,ts->tma/dot_general | solution.py:148
  216.8 8.4 %all-to-all-start.3 = ((f32[64,1,512]{2,1,0:T(1,128)}), f32[64,1,512]{2,1,0:T(1,128)S(1)}, u32[]{:S(2)}, u32[]{:S(2)}) async-start(f32[64,1,512]{2,1,0:T(1,128)} %reshape.1953), calls=%async_computation.3 | async-start | bytes 262144 | tf_op jit(solution)/shard_map/all_to_all | solution.py:237
  225.2 8.2 %scatter_custom_fusion.2 = f32[512,4096]{1,0:T(8,128)} fusion(s32[256]{0:T(256)} %bitcast.1003, f32[256,4096]{1,0:T(8,128)} %bitcast.1004, f32[]{:T(128)} %constant.54.clone.1), kind=kCustom, calls=%fused_computation.167 | custom fusion | bytes 8389120 | tf_op jit(solution)/shard_map/scatter | solution.py:217
  233.5 10.6 %reshape.1772 = f32[64,4,2,4096]{3,2,1,0:T(2,128)} reshape(f32[512,4096]{1,0:T(8,128)} %scatter_custom_fusion.2) | data formatting | bytes 16777216 | tf_op jit(solution)/shard_map/reshape | solution.py:225
  244.0 10.5 %all-to-all-start.5 = ((f32[64,4,2,4096]{3,2,1,0:T(2,128)}), f32[64,4,2,4096]{3,2,1,0:T(2,128)}, u32[]{:S(2)}, u32[]{:S(2)}) async-start(f32[64,4,2,4096]{3,2,1,0:T(2,128)} %reshape.1772), calls=%async_computation.5 | async-start | bytes 16777216 | tf_op jit(solution)/shard_map/all_to_all | solution.py:224
  257.2 178.9 %all-to-all-done.5 = f32[64,4,2,4096]{3,2,1,0:T(2,128)} async-done(((f32[64,4,2,4096]{3,2,1,0:T(2,128)}), f32[64,4,2,4096]{3,2,1,0:T(2,128)}, u32[]{:S(2)}, u32[]{:S(2)}) %all-to-all-start.5) | async-done | bytes 8388640 | tf_op jit(solution)/shard_map/all_to_all | solution.py:224
  436.1 4.2 all-to-all-start.4
  440.4 7.4 %copy.85 = f32[64,4,2,4096]{3,2,0,1:T(2,128)} copy(f32[64,4,2,4096]{3,2,1,0:T(2,128)} %all-to-all-done.5) | data formatting | bytes 16777216 | tf_op jit(solution)/shard_map/all_to_all | solution.py:224
  447.8 5.7 all-to-all-start.6
  458.8 85.5 %collective-permute-done = f32[4,1]{1,0:T(4,128)S(1)} collective-permute-done((f32[4,1]{1,0:T(4,128)S(1)}, f32[4,1]{1,0:T(4,128)S(1)}, u32[]{:S(2)}, u32[]{:S(2)}) %collective-permute-start) | collective-permute-done | bytes 48 | tf_op jit(solution)/shard_map/ppermute | solution.py:23
  548.4 7.6 %copy.86 = f32[64,4,2,4096]{3,2,1,0:T(2,128)} copy(f32[64,4,2,4096]{3,2,0,1:T(2,128)} %all-to-all-done.6) | data formatting | bytes 16777216 | tf_op jit(solution)/shard_map/all_to_all | solution.py:223
  556.0 10.9 %reshape.1773 = f32[512,4096]{1,0:T(8,128)} reshape(f32[64,4,2,4096]{3,2,1,0:T(2,128)} %copy.86) | data formatting | bytes 16777216 | tf_op jit(solution)/shard_map/reshape | solution.py:254
  566.9 9.0 %copy.87 = f32[4096,512]{1,0:T(8,128)} copy(f32[4096,512]{0,1:T(8,128)} %bitcast.916) | data formatting | bytes 16777216 | tf_op jit(solution)/shard_map/dot_general | solution.py:252
  575.9 17.0 %convolution_bitcast_fusion = f32[16,4,4,16,16]{4,0,2,3,1:T(8,128)S(1)} fusion(f32[4,16,4,16,512]{4,3,2,1,0:T(8,128)} %bitcast.915, s32[512]{0:T(512)S(1)} %eq.99), kind=kOutput, calls=%fused_computation.169 | convolution fusion | flops 402661376 | bytes 8652800 | tf_op jit(solution)/shard_map/dot_general | solution.py:252
  607.2 5.3 collective-permute-start.2
  614.5 8.4 %collective-permute-done.3 = f32[4,1]{1,0:T(4,128)S(1)} collective-permute-done((f32[4,1]{1,0:T(4,128)S(1)}, f32[4,1]{1,0:T(4,128)S(1)}, u32[]{:S(2)}, u32[]{:S(2)}) %collective-permute-start.3) | collective-permute-done | bytes 48 | tf_op jit(solution)/shard_map/ppermute | solution.py:24
  630.6 7.0 %collective-permute-done.5 = f32[4,1]{1,0:T(4,128)S(1)} collective-permute-done((f32[4,1]{1,0:T(4,128)S(1)}, f32[4,1]{1,0:T(4,128)S(1)}, u32[]{:S(2)}, u32[]{:S(2)}) %collective-permute-start.5) | collective-permute-done | bytes 48 | tf_op jit(solution)/shard_map/ppermute | solution.py:24
  641.9 3.6 collective-permute-start.7
  645.5 6.7 collective-permute-done.7
  659.9 7.0 %collective-permute-done.9 = f32[4,1]{1,0:T(4,128)S(1)} collective-permute-done((f32[4,1]{1,0:T(4,128)S(1)}, f32[4,1]{1,0:T(4,128)S(1)}, u32[]{:S(2)}, u32[]{:S(2)}) %collective-permute-start.9) | collective-permute-done | bytes 48 | tf_op jit(solution)/shard_map/ppermute | solution.py:24
  674.6 7.0 %collective-permute-done.11 = f32[4,1]{1,0:T(4,128)S(1)} collective-permute-done((f32[4,1]{1,0:T(4,128)S(1)}, f32[4,1]{1,0:T(4,128)S(1)}, u32[]{:S(2)}, u32[]{:S(2)}) %collective-permute-start.11) | collective-permute-done | bytes 48 | tf_op jit(solution)/shard_map/ppermute | solution.py:24
  (519 shorter events, 138.4 us)
Async XLA Ops:
  0.6 38.2 %copy-start = (f32[4,64,512]{2,1,0:T(8,128)S(1)}, f32[4,64,512]{2,1,0:T(8,128)}, u32[]{:S(2)}) copy-start(f32[4,64,512]{2,1,0:T(8,128)} %param.13) | copy-start | bytes 1572868
  0.6 39.1 %copy-start.1 = (f32[64,512]{1,0:T(8,128)S(1)}, f32[64,512]{1,0:T(8,128)}, u32[]{:S(2)}) copy-start(f32[64,512]{1,0:T(8,128)} %param.14) | copy-start | bytes 393220
  0.7 39.2 %copy-start.2 = (s32[64,512]{1,0:T(8,128)S(1)}, s32[64,512]{1,0:T(8,128)}, u32[]{:S(2)}) copy-start(s32[64,512]{1,0:T(8,128)} %param.16) | copy-start | bytes 393220
  0.7 39.2 %copy-start.3 = (f32[64,512]{1,0:T(8,128)S(1)}, f32[64,512]{1,0:T(8,128)}, u32[]{:S(2)}) copy-start(f32[64,512]{1,0:T(8,128)} %param.15) | copy-start | bytes 393220
  0.7 39.9 %copy-start.21 = (s32[4]{0:T(128)S(1)}, s32[4]{0:T(128)}, u32[]{:S(2)}) copy-start(s32[4]{0:T(128)} %param.17) | copy-start | bytes 52
  24.5 36.6 %all-to-all-start = ((f32[256,4,256]{2,1,0:T(4,128)}), f32[256,4,256]{2,1,0:T(4,128)S(1)}, u32[]{:S(2)}, u32[]{:S(2)}) async-start(f32[256,4,256]{2,1,0:T(4,128)} %stack.76), calls=%async_computation | async-start | bytes 2097152 | tf_op jit(solution)/shard_map/all_to_all | solution.py:198
  61.1 155.7 %all-to-all-start.2 = ((s32[4,1,128]{2,1,0:T(1,128)}), s32[4,1,128]{2,1,0:T(1,128)}, u32[]{:S(2)}, u32[]{:S(2)}) async-start(s32[4,1,128]{2,1,0:T(1,128)} %reshape.1951), calls=%async_computation.2 | async-start | bytes 4096 | tf_op jit(solution)/shard_map/all_to_all | solution.py:183
  95.8 0.6 copy-start.5
  95.8 0.6 copy-start.11
  127.1 0.6 copy-start.5
  127.1 0.6 copy-start.6
  127.1 0.6 copy-start.11
  158.4 0.6 copy-start.5
  158.5 0.6 copy-start.11
  189.7 0.6 copy-start.5
  189.8 0.6 copy-start.11
  216.8 27.3 %all-to-all-start.3 = ((f32[64,1,512]{2,1,0:T(1,128)}), f32[64,1,512]{2,1,0:T(1,128)S(1)}, u32[]{:S(2)}, u32[]{:S(2)}) async-start(f32[64,1,512]{2,1,0:T(1,128)} %reshape.1953), calls=%async_computation.3 | async-start | bytes 262144 | tf_op jit(solution)/shard_map/all_to_all | solution.py:237
  244.0 192.1 %all-to-all-start.5 = ((f32[64,4,2,4096]{3,2,1,0:T(2,128)}), f32[64,4,2,4096]{3,2,1,0:T(2,128)}, u32[]{:S(2)}, u32[]{:S(2)}) async-start(f32[64,4,2,4096]{3,2,1,0:T(2,128)} %reshape.1772), calls=%async_computation.5 | async-start | bytes 16777216 | tf_op jit(solution)/shard_map/all_to_all | solution.py:224
  436.1 11.6 %all-to-all-start.4 = ((f32[4,1,8192]{2,1,0:T(1,128)}), f32[4,1,8192]{2,1,0:T(1,128)S(1)}, u32[]{:S(2)}, u32[]{:S(2)}) async-start(f32[4,1,8192]{2,1,0:T(1,128)} %reshape.1955), calls=%async_computation.4 | async-start | bytes 262144 | tf_op jit(solution)/shard_map/all_to_all | solution.py:236
  447.8 100.6 %all-to-all-start.6 = ((f32[64,4,2,4096]{3,2,0,1:T(2,128)}), f32[64,4,2,4096]{3,2,0,1:T(2,128)}, u32[]{:S(2)}, u32[]{:S(2)}) async-start(f32[64,4,2,4096]{3,2,0,1:T(2,128)} %copy.85), calls=%async_computation.6 | async-start | bytes 16777216 | tf_op jit(solution)/shard_map/all_to_all | solution.py:223
  453.4 90.9 %collective-permute-start = (f32[4,1]{1,0:T(4,128)S(1)}, f32[4,1]{1,0:T(4,128)S(1)}, u32[]{:S(2)}, u32[]{:S(2)}) collective-permute-start(f32[4,1]{1,0:T(4,128)S(1)} %broadcast.743), channel_id=1, source_target_pairs={{0,1},{1,2},{2,3},{3,4},{4,5},{5,6},{6,7},{7,8},{8,9},{9,10},{10,1... | collective-permute-start | bytes 56 | tf_op jit(solution)/shard_map/ppermute | solution.py:23
  456.8 87.5 %collective-permute-start.1 = (f32[4,1]{1,0:T(4,128)S(1)}, f32[4,1]{1,0:T(4,128)S(1)}, u32[]{:S(2)}, u32[]{:S(2)}) collective-permute-start(f32[4,1]{1,0:T(4,128)S(1)} %broadcast.743), channel_id=1, source_target_pairs={{1,0},{2,1},{3,2},{4,3},{5,4},{6,5},{7,6},{8,7},{9,8},{10,9},{11,1... | collective-permute-start | bytes 56 | tf_op jit(solution)/shard_map/ppermute | solution.py:24
  607.2 7.3 %collective-permute-start.2 = (f32[4,1]{1,0:T(4,128)S(1)}, f32[4,1]{1,0:T(4,128)S(1)}, u32[]{:S(2)}, u32[]{:S(2)}) collective-permute-start(f32[4,1]{1,0:T(4,128)S(1)} %get-tuple-element.276), channel_id=1, source_target_pairs={{0,1},{1,2},{2,3},{3,4},{4,5},{5,6},{6,7},{7,8},{8,9},{9,10},{10,1... | collective-permute-start | bytes 56 | tf_op jit(solution)/shard_map/ppermute | solution.py:23
  612.6 10.3 %collective-permute-start.3 = (f32[4,1]{1,0:T(4,128)S(1)}, f32[4,1]{1,0:T(4,128)S(1)}, u32[]{:S(2)}, u32[]{:S(2)}) collective-permute-start(f32[4,1]{1,0:T(4,128)S(1)} %get-tuple-element.277), channel_id=1, source_target_pairs={{1,0},{2,1},{3,2},{4,3},{5,4},{6,5},{7,6},{8,7},{9,8},{10,9},{11,1... | collective-permute-start | bytes 56 | tf_op jit(solution)/shard_map/ppermute | solution.py:24
  625.3 5.3 collective-permute-start.4
  627.2 10.3 %collective-permute-start.5 = (f32[4,1]{1,0:T(4,128)S(1)}, f32[4,1]{1,0:T(4,128)S(1)}, u32[]{:S(2)}, u32[]{:S(2)}) collective-permute-start(f32[4,1]{1,0:T(4,128)S(1)} %get-tuple-element.275), channel_id=1, source_target_pairs={{1,0},{2,1},{3,2},{4,3},{5,4},{6,5},{7,6},{8,7},{9,8},{10,9},{11,1... | collective-permute-start | bytes 56 | tf_op jit(solution)/shard_map/ppermute | solution.py:24
  639.9 5.5 collective-permute-start.6
  641.9 10.3 %collective-permute-start.7 = (f32[4,1]{1,0:T(4,128)S(1)}, f32[4,1]{1,0:T(4,128)S(1)}, u32[]{:S(2)}, u32[]{:S(2)}) collective-permute-start(f32[4,1]{1,0:T(4,128)S(1)} %get-tuple-element.273), channel_id=1, source_target_pairs={{1,0},{2,1},{3,2},{4,3},{5,4},{6,5},{7,6},{8,7},{9,8},{10,9},{11,1... | collective-permute-start | bytes 56 | tf_op jit(solution)/shard_map/ppermute | solution.py:24
  654.6 5.3 collective-permute-start.8
  656.5 10.3 %collective-permute-start.9 = (f32[4,1]{1,0:T(4,128)S(1)}, f32[4,1]{1,0:T(4,128)S(1)}, u32[]{:S(2)}, u32[]{:S(2)}) collective-permute-start(f32[4,1]{1,0:T(4,128)S(1)} %get-tuple-element.271), channel_id=1, source_target_pairs={{1,0},{2,1},{3,2},{4,3},{5,4},{6,5},{7,6},{8,7},{9,8},{10,9},{11,1... | collective-permute-start | bytes 56 | tf_op jit(solution)/shard_map/ppermute | solution.py:24
  669.3 5.3 collective-permute-start.10
  671.2 10.3 %collective-permute-start.11 = (f32[4,1]{1,0:T(4,128)S(1)}, f32[4,1]{1,0:T(4,128)S(1)}, u32[]{:S(2)}, u32[]{:S(2)}) collective-permute-start(f32[4,1]{1,0:T(4,128)S(1)} %get-tuple-element.269), channel_id=1, source_target_pairs={{1,0},{2,1},{3,2},{4,3},{5,4},{6,5},{7,6},{8,7},{9,8},{10,9},{11,1... | collective-permute-start | bytes 56 | tf_op jit(solution)/shard_map/ppermute | solution.py:24
  (56 other events, 31.7 us)
